TPU v7x, 32 devices: a whole 2x2x4 slice. The times are simulated.
32 devices in a mesh: seq: 16 (over z, y, core), dp: 2 (over x).
Axes of the slice: x: 2, y: 2, z: 4, core: 2. Of those that a mesh axis runs over, the one named last changes fastest.
Arguments:
- queries: bfloat16 [2, 4096, 2048], P('dp', 'seq'), may hold values from -6 to 6
- key_rows: bfloat16 [2, 4096, 2048], P('dp', 'seq'), may hold values from -6 to 6
- value_rows: bfloat16 [2, 4096, 2048], P('dp', 'seq'), may hold values from -6 to 6
- out_grad: bfloat16 [2, 4096, 2048], P('dp', 'seq'), may hold values from -6 to 6
- out_weight: bfloat16 [2048, 2048], P('seq', 'dp'), may hold values from -0.125 to 0.125
Outputs:
- query_grad: bfloat16 [2, 4096, 2048], P('dp', 'seq')
- key_grad: bfloat16 [2, 4096, 2048], P('dp', 'seq')
- value_grad: bfloat16 [2, 4096, 2048], P('dp', 'seq')
- weight_grad: float32 [2048, 2048], P('seq', 'dp')
All inputs are finite; a program needn't handle non-finite values.
Results may differ from a plain program's by a relative error of at most 0.014.
Values may be sent and summed in bfloat16 or wider, within the bound.
A program may use at most 192 MiB of HBM per device.

v0:
```python
import math
import jax
import jax.numpy as jnp
from jax import lax
from jax.sharding import PartitionSpec as P

HEADS = 16
HEAD = 128
HD = 2048


def prefix_2(part, axis, combine, identity, reverse):
    count = lax.axis_size(axis)
    place = lax.axis_index(axis)
    ahead = count - 1 - place if reverse else place
    gathered = lax.all_gather(part, axis)
    state = jnp.zeros_like(part) + jnp.asarray(identity, part.dtype)

    def one(step, state):
        source = count - 1 - step if reverse else step
        return combine(state, lax.dynamic_index_in_dim(gathered, source, 0, False))

    return lax.fori_loop(0, ahead, one, state)


def add_sums(earlier, later):
    return earlier + later


def shards(queries, key_rows, value_rows, out_grad, out_weight):
    tokens_dev = queries.shape[1]
    seq_devices = lax.axis_size("seq")
    data_devices = lax.axis_size("dp")
    seq_length = tokens_dev * seq_devices
    seq_count = queries.shape[0] * data_devices
    score_scale = 1.0 / math.sqrt(HEAD * seq_length)
    grad_scale = 1.0 / math.sqrt(seq_count * seq_length)
    query_flat = queries[0]
    grad_flat = out_grad[0]
    query_h = query_flat.reshape(tokens_dev, HEADS, HEAD)
    key_h = key_rows[0].reshape(tokens_dev, HEADS, HEAD)
    value_h = value_rows[0].reshape(tokens_dev, HEADS, HEAD)
    row_ids = lax.broadcasted_iota(jnp.int32, (tokens_dev, tokens_dev), 0)
    col_ids = lax.broadcasted_iota(jnp.int32, (tokens_dev, tokens_dev), 1)
    causal = (row_ids >= col_ids).astype(jnp.float32)
    empty_state = jnp.zeros((HEADS, HEAD, HEAD), jnp.float32)
    kv_local = jnp.einsum("shd,she->hde", key_h, value_h, preferred_element_type=jnp.float32)
    wide_weight = lax.all_gather(out_weight, "dp", axis=1, tiled=True)
    head_grad = lax.dot_general(
        grad_flat,
        lax.all_gather(wide_weight, "seq", axis=0, tiled=True),
        (((1,), (1,)), ((), ())),
        preferred_element_type=jnp.float32,
    ).astype(jnp.bfloat16)
    grad_h = head_grad.reshape(tokens_dev, HEADS, HEAD)
    query_dout = jnp.einsum("thd,the->hde", query_h, grad_h, preferred_element_type=jnp.float32)
    prefix = prefix_2(kv_local, "seq", add_sums, empty_state, False)
    suffix = prefix_2(query_dout, "seq", add_sums, empty_state, True)
    prefix_scaled = (score_scale * prefix).astype(jnp.bfloat16)
    suffix_scaled = (score_scale * suffix).astype(jnp.bfloat16)
    scores = (
        score_scale
        * jnp.einsum("thd,shd->hts", query_h, key_h, preferred_element_type=jnp.float32)
        * causal
    ).astype(jnp.bfloat16)
    attended = jnp.einsum("hts,shd->thd", scores, value_h, preferred_element_type=jnp.float32)
    attended = attended + jnp.einsum(
        "thd,hde->the", query_h, prefix_scaled, preferred_element_type=jnp.float32
    )
    attended = attended.astype(jnp.bfloat16).reshape(tokens_dev, HD)
    row_sums = lax.psum_scatter(
        (
            grad_scale
            * lax.dot_general(
                attended, grad_flat, (((0,), (0,)), ((), ())), preferred_element_type=jnp.float32
            )
        ).astype(jnp.bfloat16),
        "seq",
        scatter_dimension=0,
        tiled=True,
    )
    weight_grad = lax.psum_scatter(row_sums, "dp", scatter_dimension=1, tiled=True).astype(
        jnp.float32
    )
    grad_scores = (
        score_scale
        * jnp.einsum("the,she->hts", grad_h, value_h, preferred_element_type=jnp.float32)
        * causal
    ).astype(jnp.bfloat16)
    query_g = jnp.einsum("hts,shd->thd", grad_scores, key_h, preferred_element_type=jnp.float32)
    query_g = query_g + jnp.einsum(
        "the,hde->thd", grad_h, prefix_scaled, preferred_element_type=jnp.float32
    )
    key_g = jnp.einsum("hts,thd->shd", grad_scores, query_h, preferred_element_type=jnp.float32)
    key_g = key_g + jnp.einsum(
        "she,hde->shd", value_h, suffix_scaled, preferred_element_type=jnp.float32
    )
    value_g = jnp.einsum("hts,the->she", scores, grad_h, preferred_element_type=jnp.float32)
    value_g = value_g + jnp.einsum(
        "shd,hde->she", key_h, suffix_scaled, preferred_element_type=jnp.float32
    )
    query_grad = query_g.astype(jnp.bfloat16).reshape(1, tokens_dev, HD)
    key_grad = key_g.astype(jnp.bfloat16).reshape(1, tokens_dev, HD)
    value_grad = value_g.astype(jnp.bfloat16).reshape(1, tokens_dev, HD)
    return (query_grad, key_grad, value_grad, weight_grad)


def solution(mesh):
    return jax.shard_map(
        shards,
        mesh=mesh,
        in_specs=(
            P("dp", "seq", None),
            P("dp", "seq", None),
            P("dp", "seq", None),
            P("dp", "seq", None),
            P("seq", "dp"),
        ),
        out_specs=(
            P("dp", "seq", None),
            P("dp", "seq", None),
            P("dp", "seq", None),
            P("seq", "dp"),
        ),
        check_vma=False,
    )
```

profile of v0, /device:TPU:0, one launch (start us, length us, event | category | flops | bytes accessed | tf_op | source)
XLA Modules:
  0.0 536.6 jit_solution(13903750123057285457)
XLA Ops:
  7.2 1.6 copy.56
  8.8 1.8 copy.57
  10.6 1.5 fusion.5
  12.2 1.5 copy.58
  13.7 0.7 multiply_convert_fusion.1
  14.6 1.3 copy-done.8
  16.0 2.2 fusion.22
  18.2 123.7 %all-gather.8.cloned.1.call-done = f32[256,128,128]{2,1,0:T(8,128)} async-done(((f32[16,128,128]{2,1,0:T(8,128)}), f32[256,128,128]{2,1,0:T(8,128)}) %all-gather.8.cloned.1.call-update) | async-done | bytes 16777232 | tf_op jit(solution)/shard_map/all_gather | solution.py:16
  142.0 2.5 fusion
  144.5 5.7 %multiply_convert_fusion = bf16[2048,2048]{1,0:T(8,128)(2,1)} fusion(bf16[256,2048]{0,1:T(8,128)(2,1)S(1)} %bitcast.84, bf16[1,256,2048]{2,1,0:T(8,128)(2,1)S(1)} %copy-done), kind=kOutput, calls=%fused_computation.2 | convolution fusion | flops 2155872256 | bytes 10485760 | tf_op jit(solution)/shard_map/dot_general | solution.py:74
  150.2 10.2 %all_gather.18 = bf16[128,2048]{1,0:T(8,128)(2,1)} all-gather(bf16[128,1024]{1,0:T(8,128)(2,1)} %param.13), channel_id=1, replica_groups=mesh['seq'=16,'dp'=2] {'dp'}, dimensions={1}, use_global_device_ids=true | all-gather | bytes 786432 | tf_op jit(solution)/shard_map/all_gather | solution.py:48
  160.5 115.1 %reduce-scatter.3.cloned.1.call-done = bf16[128,2048]{1,0:T(8,128)(2,1)} async-done(((bf16[2048,2048]{1,0:T(8,128)(2,1)}), bf16[128,2048]{1,0:T(8,128)(2,1)}) %reduce-scatter.3.cloned.1.call-update) | async-done | bytes 524304 | tf_op jit(solution)/shard_map/reduce_scatter | solution.py:71
  275.6 0.2 all-gather.10.cloned.1.call-start
  275.9 76.6 %all-gather.6.cloned.1.call-done = bf16[2048,2048]{1,0:T(8,128)(2,1)} async-done(((bf16[128,2048]{1,0:T(8,128)(2,1)}), bf16[2048,2048]{1,0:T(8,128)(2,1)}) %all-gather.6.cloned.1.call-update) | async-done | bytes 8388624 | tf_op jit(solution)/shard_map/all_gather | solution.py:51
  352.5 6.8 %convolution_convert_fusion = bf16[256,2048]{1,0:T(8,128)(2,1)} fusion(bf16[2048,2048]{1,0:T(8,128)(2,1)} %all-gather.6.cloned.1.call-done, bf16[1,256,2048]{2,1,0:T(8,128)(2,1)S(1)} %copy-done), kind=kOutput, calls=%fused_computation.5 | convolution fusion | flops 2148007936 | bytes 10485760 | tf_op jit(solution)/shard_map/dot_general | solution.py:49
  359.2 2.3 copy.55
  361.6 2.7 convolution_bitcast_fusion
  364.2 2.7 copy.40
  366.9 2.0 multiply_convert_fusion.2
  369.0 0.8 fusion.7
  369.8 0.4 copy-done.6
  370.2 1.9 fusion.11
  372.0 0.8 copy-done.9
  372.9 1.8 fusion.21
  374.6 1.4 fusion.2
  376.1 2.3 copy.50
  378.4 1.8 convert_element_type.52
  380.2 116.4 %all-gather.10.cloned.1.call-done = f32[256,128,128]{2,1,0:T(8,128)} async-done(((f32[16,128,128]{2,1,0:T(8,128)}), f32[256,128,128]{2,1,0:T(8,128)}) %all-gather.10.cloned.1.call-update) | async-done | bytes 16777232 | tf_op jit(solution)/shard_map/all_gather | solution.py:16
  496.7 22.7 %while.23 = (s32[]{:T(128)}, f32[16,128,128]{2,1,0:T(8,128)S(1)}, s32[]{:T(128)}, f32[16,16,128,128]{3,2,1,0:T(8,128)}, s32[]{:T(128)}, /*index=5*/s32[]{:T(128)}, s32[]{:T(128)}, s32[]{:T(128)}) while((s32[]{:T(128)}, f32[16,128,128]{2,1,0:T(8,128)S(1)}, s32[]{:T(128)}, f32[16,16,128,128]{3,2,1,0:T(8,128)}, s32[]{:T(128)}, ...), condition=%wide.region_3.4_spmd, body=%wide.region_2.3_spmd.sunk | while | flops 262150 | bytes 3145871 | solution.py:23
  496.7 1.5 bitcast_add_fusion.8
  498.2 1.5 bitcast_add_fusion.8
  499.7 1.5 bitcast_add_fusion.8
  501.2 1.5 bitcast_add_fusion.8
  502.7 1.5 bitcast_add_fusion.8
  504.2 1.5 bitcast_add_fusion.8
  505.8 1.5 bitcast_add_fusion.8
  507.3 1.5 bitcast_add_fusion.8
  508.8 1.5 bitcast_add_fusion.8
  510.3 1.5 bitcast_add_fusion.8
  511.8 1.5 bitcast_add_fusion.8
  513.3 1.5 bitcast_add_fusion.8
  514.8 1.5 bitcast_add_fusion.8
  516.3 1.5 bitcast_add_fusion.8
  517.8 1.5 bitcast_add_fusion.8
  519.3 3.0 fusion.1
  522.3 2.3 copy.51
  524.6 3.2 add_convert_fusion
  527.8 2.3 copy.52
  (31 shorter events, 0.7 us)
Async XLA Ops:
  7.2 137.3 %copy-start = (bf16[1,256,2048]{2,1,0:T(8,128)(2,1)S(1)}, bf16[1,256,2048]{2,1,0:T(8,128)(2,1)}, u32[]{:S(2)}) copy-start(bf16[1,256,2048]{2,1,0:T(8,128)(2,1)} %param.12) | copy-start | bytes 3145732
  7.2 134.7 %all-gather.8.cloned.1.call-start = ((), (), s32[]{:S(2)}) async-start(), calls=%async_computation.5 | async-start | bytes 17825792 | tf_op jit(solution)/shard_map/all_gather | solution.py:16
  8.8 5.6 %copy-start.2 = (bf16[1,256,2048]{1,2,0:T(8,128)(2,1)}, bf16[1,256,2048]{1,2,0:T(8,128)(2,1)S(1)}, u32[]{:S(2)}) copy-start(bf16[1,256,2048]{1,2,0:T(8,128)(2,1)S(1)} %copy.56) | copy-start | bytes 3145732
  12.1 263.5 %reduce-scatter.3.cloned.1.call-start = ((), (), s32[]{:S(2)}) async-start(), calls=%async_computation.3 | async-start | bytes 8912896 | tf_op jit(solution)/shard_map/reduce_scatter | solution.py:71
  13.6 1.0 copy-start.4
  14.6 1.3 copy-start.8
  150.2 202.3 %all-gather.6.cloned.1.call-start = ((), (), s32[]{:S(2)}) async-start(), calls=%async_computation.2 | async-start | bytes 8912896 | tf_op jit(solution)/shard_map/all_gather | solution.py:51
  160.5 217.9 %reduce-scatter.5.cloned.1.call-start = ((), (), s32[]{:S(2)}) async-start(), calls=%async_computation.4 | async-start | bytes 786432 | tf_op jit(solution)/shard_map/reduce_scatter | solution.py:82
  275.6 220.9 %all-gather.10.cloned.1.call-start = ((), (), s32[]{:S(2)}) async-start(), calls=%async_computation.6 | async-start | bytes 17825792 | tf_op jit(solution)/shard_map/all_gather | solution.py:16
  359.2 2.4 copy-start.5
  364.2 2.7 copy-start.3
  368.9 1.2 copy-start.6
  370.2 1.9 copy-start.7
  370.2 2.7 copy-start.9
  524.6 5.5 %copy-start.1 = (bf16[1,256,2048]{2,1,0:T(8,128)(2,1)S(1)}, bf16[1,256,2048]{2,1,0:T(8,128)(2,1)}, u32[]{:S(2)}) copy-start(bf16[1,256,2048]{2,1,0:T(8,128)(2,1)} %param.12) | copy-start | bytes 3145732
Sparse Core Ops, SparseCore 0:
  12.2 129.5 all-gather.7
  150.3 125.2 reduce-scatter.2
  277.8 74.6 all-gather.5
  354.6 12.7 reduce-scatter.4
  369.6 126.8 all-gather.9
where the time goes:
time: 538 us; the launch traced here: 537 us
  waiting for transfers between devices  432 us (80%)
  matrix products  36 us (7%)
  other arithmetic  24.1 us (4%)
  local copies, waits for them, and re-layouts  19.7 us (4%)
  between operations  13.9 us (3%)
  blocking collectives  10.2 us (2%)
    all_gather x2, waiting for transfers between devices, prefix_2(): gathered = lax.all_gather(part, axis)  240 us
    reduce_scatter x1, waiting for transfers between devices, shards(): lax.psum_scatter((grad_scale * lax.dot_general(attended, grad_flat, (((0,...  115 us
    all_gather x1, waiting for transfers between devices, shards(): lax.all_gather(wide_weight, 'seq', axis=0, tiled=True)  76.6 us
    add x15, other arithmetic, add_sums(): return earlier + later  22.3 us
    unnamed x25, local copies, waits for them, and re-layouts  12.9 us
  transfers between devices with their start and end apart: 5, of which 4 were waited for; matrix products, arithmetic and copies ran while one was open for 6% of the time, Pallas kernels for 0%

commit v1 on v0

--- a/solution.py
+++ b/solution.py
@@ -7,6 +7,24 @@
 HEADS = 16
 HEAD = 128
 HD = 2048
+
+
+def ring_gather(shard, axis, dim):
+    ways, here, step = (lax.axis_size(axis), lax.axis_index(axis), shard.shape[dim])
+    shape = [n * ways if d == dim else n for d, n in enumerate(shard.shape)]
+    full = lax.dynamic_update_slice_in_dim(
+        jnp.zeros(shape, shard.dtype), shard, here * step, axis=dim
+    )
+    going_up = going_down = shard
+    for far in range(1, ways // 2 + 1):
+        going_up = lax.ppermute(going_up, axis, [(d, (d + 1) % ways) for d in range(ways)])
+        full = lax.dynamic_update_slice_in_dim(full, going_up, (here - far) % ways * step, axis=dim)
+        if 2 * far < ways:
+            going_down = lax.ppermute(going_down, axis, [(d, (d - 1) % ways) for d in range(ways)])
+            full = lax.dynamic_update_slice_in_dim(
+                full, going_down, (here + far) % ways * step, axis=dim
+            )
+    return full
 
 
 def prefix_2(part, axis, combine, identity, reverse):
@@ -48,7 +66,7 @@
     wide_weight = lax.all_gather(out_weight, "dp", axis=1, tiled=True)
     head_grad = lax.dot_general(
         grad_flat,
-        lax.all_gather(wide_weight, "seq", axis=0, tiled=True),
+        ring_gather(wide_weight, "seq", 0),
         (((1,), (1,)), ((), ())),
         preferred_element_type=jnp.float32,
     ).astype(jnp.bfloat16)

time: 538 us -> 494 us (0.918)
  waiting for transfers between devices: 432 us -> 305 us
  starting transfers between devices: 0.38 us -> 61.6 us
  local copies, waits for them, and re-layouts: 19.7 us -> 43.9 us
    reduce_scatter x1, waiting for transfers between devices: 115 us -> 0.01 us  [shards(): lax.psum_scatter((grad_scale * lax.dot_general(attended, grad_flat, (((0,...]
    all_gather x1 -> x0, waiting for transfers between devices: 76.6 us -> none  [shards(): lax.all_gather(wide_weight, 'seq', axis=0, tiled=True)]
    ppermute x0 -> x15, waiting for transfers between devices: none -> 67.4 us  [the longest x8 55.6 us: ring_gather(): lax.ppermute(going_up, axis, [(d, (d + 1) % ways) for d in range(ways)])]
    ppermute x0 -> x15, starting transfers between devices: none -> 61.5 us  [the longest x7 60.9 us: ring_gather(): lax.ppermute(going_down, axis, [(d, (d - 1) % ways) for d in range(ways)])]
    dynamic_update_slice x0 -> x16, local copies, waits for them, and re-layouts: none -> 20.8 us  [the longest x8 11 us: ring_gather(): lax.dynamic_update_slice_in_dim(full, going_up, (here - far) % ways * ste...]
    unnamed x25 -> x31, local copies, waits for them, and re-layouts: 12.9 us -> 14.4 us
  transfers between devices with their start and end apart: 5 -> 19, of which waited for: 4 -> 14; matrix products, arithmetic and copies ran while one was open for 6% -> 17% of each run, Pallas kernels for 0% -> 0%
where the time goes in v1:
time: 494 us; the launch traced here: 492 us
  waiting for transfers between devices  305 us (62%)
  starting transfers between devices  61.6 us (12%)
  local copies, waits for them, and re-layouts  43.9 us (9%)
  matrix products  34.6 us (7%)
  other arithmetic  24.1 us (5%)
  between operations  14 us (3%)
  blocking collectives  9.31 us (2%)
    all_gather x2, waiting for transfers between devices, prefix_2(): gathered = lax.all_gather(part, axis)  237 us
    ppermute x7, starting transfers between devices, ring_gather(): lax.ppermute(going_down, axis, [(d, (d - 1) % ways) for d in range(ways)])  60.9 us
    ppermute x8, waiting for transfers between devices, ring_gather(): lax.ppermute(going_up, axis, [(d, (d + 1) % ways) for d in range(ways)])  55.6 us
    add x15, other arithmetic, add_sums(): return earlier + later  22.3 us
    unnamed x31, local copies, waits for them, and re-layouts  14.4 us
    ppermute x7, waiting for transfers between devices, ring_gather(): lax.ppermute(going_down, axis, [(d, (d - 1) % ways) for d in range(ways)])  11.8 us
    dynamic_update_slice x8, local copies, waits for them, and re-layouts, ring_gather(): lax.dynamic_update_slice_in_dim(full, going_up, (here - far) % ways * ste...  11 us
  transfers between devices with their start and end apart: 19, of which 14 were waited for; matrix products, arithmetic and copies ran while one was open for 17% of the time, Pallas kernels for 0%

profile of v1, /device:TPU:0, one launch (start us, length us, event | category | flops | bytes accessed | tf_op | source)
XLA Modules:
  0.0 492.4 jit_solution(18183826916400708576)
XLA Ops:
  7.2 1.6 copy.53
  8.8 1.8 copy.54
  16.7 2.2 fusion.22
  18.9 123.0 %all-gather.5.cloned.1.call-done = f32[256,128,128]{2,1,0:T(8,128)} async-done(((f32[16,128,128]{2,1,0:T(8,128)}), f32[256,128,128]{2,1,0:T(8,128)}) %all-gather.5.cloned.1.call-update) | async-done | bytes 16777232 | tf_op jit(solution)/shard_map/all_gather | solution.py:34
  142.0 2.5 fusion
  144.5 5.6 %multiply_convert_fusion = bf16[2048,2048]{1,0:T(8,128)(2,1)} fusion(bf16[256,2048]{0,1:T(8,128)(2,1)S(1)} %bitcast.86, bf16[1,256,2048]{2,1,0:T(8,128)(2,1)S(1)} %copy-done), kind=kOutput, calls=%fused_computation.2 | convolution fusion | flops 2155872256 | bytes 10485760 | tf_op jit(solution)/shard_map/dot_general | solution.py:92
  150.2 9.3 %all_gather.15 = bf16[128,2048]{1,0:T(8,128)(2,1)S(1)} all-gather(bf16[128,1024]{1,0:T(8,128)(2,1)} %param.13), channel_id=1, replica_groups=mesh['seq'=16,'dp'=2] {'dp'}, dimensions={1}, use_global_device_ids=true | all-gather | bytes 786432 | tf_op jit(solution)/shard_map/all_gather | solution.py:66
  160.3 22.6 %collective-permute-start.1 = (bf16[128,2048]{1,0:T(8,128)(2,1)S(1)}, bf16[128,2048]{1,0:T(8,128)(2,1)S(1)}, u32[]{:S(2)}, u32[]{:S(2)}) collective-permute-start(bf16[128,2048]{1,0:T(8,128)(2,1)S(1)} %all_gather.15), channel_id=1, source_target_pairs={{0,30},{2,0},{4,2},{6,4},{8,6},{10,8},{12,10},{14,12},{16,14},{18,... | collective-permute-start | bytes 1572872 | tf_op jit(solution)/shard_map/ppermute | solution.py:23
  182.9 6.2 %collective-permute-done = bf16[128,2048]{1,0:T(8,128)(2,1)S(1)} collective-permute-done((bf16[128,2048]{1,0:T(8,128)(2,1)S(1)}, bf16[128,2048]{1,0:T(8,128)(2,1)S(1)}, u32[]{:S(2)}, u32[]{:S(2)}) %collective-permute-start) | collective-permute-done | bytes 524320 | tf_op jit(solution)/shard_map/ppermute | solution.py:20
  190.4 4.7 collective-permute-start.3
  195.1 5.5 %collective-permute-done.2 = bf16[128,2048]{1,0:T(8,128)(2,1)} collective-permute-done((bf16[128,2048]{1,0:T(8,128)(2,1)S(1)}, bf16[128,2048]{1,0:T(8,128)(2,1)}, u32[]{:S(2)}, u32[]{:S(2)}) %collective-permute-start.2) | collective-permute-done | bytes 524320 | tf_op jit(solution)/shard_map/ppermute | solution.py:20
  201.8 4.8 collective-permute-start.5
  206.6 14.4 %collective-permute-done.4 = bf16[128,2048]{1,0:T(8,128)(2,1)} collective-permute-done((bf16[128,2048]{1,0:T(8,128)(2,1)}, bf16[128,2048]{1,0:T(8,128)(2,1)}, u32[]{:S(2)}, u32[]{:S(2)}) %collective-permute-start.4) | collective-permute-done | bytes 524320 | tf_op jit(solution)/shard_map/ppermute | solution.py:20
  221.1 4.3 broadcast_in_dim.8
  226.2 2.0 constant_dynamic-update-slice_fusion.14
  228.2 4.9 collective-permute-start.7
  233.1 1.9 constant_dynamic-update-slice_fusion.13
  235.0 9.5 %collective-permute-done.6 = bf16[128,2048]{1,0:T(8,128)(2,1)} collective-permute-done((bf16[128,2048]{1,0:T(8,128)(2,1)}, bf16[128,2048]{1,0:T(8,128)(2,1)}, u32[]{:S(2)}, u32[]{:S(2)}) %collective-permute-start.6) | collective-permute-done | bytes 524320 | tf_op jit(solution)/shard_map/ppermute | solution.py:20
  244.5 1.9 constant_dynamic-update-slice_fusion.12
  246.4 1.9 constant_dynamic-update-slice_fusion.11
  248.3 4.4 collective-permute-start.9
  252.7 1.9 constant_dynamic-update-slice_fusion.10
  254.6 2.8 collective-permute-done.8
  257.4 1.9 constant_dynamic-update-slice_fusion.9
  259.3 1.9 constant_dynamic-update-slice_fusion.8
  261.2 14.7 %collective-permute-start.11 = (bf16[128,2048]{1,0:T(8,128)(2,1)S(1)}, bf16[128,2048]{1,0:T(8,128)(2,1)S(1)}, u32[]{:S(2)}, u32[]{:S(2)}) collective-permute-start(bf16[128,2048]{1,0:T(8,128)(2,1)S(1)} %collective-permute-done.9), channel_id=1, source_target_pairs={{0,30},{2,0},{4,2},{6,4},{8,6},{10,8},{12,10},{14,12},{16,14},{18,... | collective-permute-start | bytes 1572872 | tf_op jit(solution)/shard_map/ppermute | solution.py:23
  276.7 2.3 collective-permute-done.10
  280.8 1.8 collective-permute-done.11
  282.6 4.7 collective-permute-start.13
  288.1 4.0 collective-permute-done.12
  293.8 8.3 %collective-permute-done.13 = bf16[128,2048]{1,0:T(8,128)(2,1)S(1)} collective-permute-done((bf16[128,2048]{1,0:T(8,128)(2,1)S(1)}, bf16[128,2048]{1,0:T(8,128)(2,1)S(1)}, u32[]{:S(2)}, u32[]{:S(2)}) %collective-permute-start.13) | collective-permute-done | bytes 524320 | tf_op jit(solution)/shard_map/ppermute | solution.py:23
  303.0 10.7 %collective-permute-done.14 = bf16[128,2048]{1,0:T(8,128)(2,1)S(1)} collective-permute-done((bf16[128,2048]{1,0:T(8,128)(2,1)S(1)}, bf16[128,2048]{1,0:T(8,128)(2,1)S(1)}, u32[]{:S(2)}, u32[]{:S(2)}) %collective-permute-start.14) | collective-permute-done | bytes 524320 | tf_op jit(solution)/shard_map/ppermute | solution.py:20
  314.5 5.9 %convolution_convert_fusion = bf16[2048,256]{1,0:T(8,128)(2,1)S(1)} fusion(bf16[2048,2048]{1,0:T(8,128)(2,1)} %constant_dynamic-update-slice_fusion, bf16[1,256,2048]{2,1,0:T(8,128)(2,1)S(1)} %copy-done), kind=kOutput, calls=%fused_computation.5 | convolution fusion | flops 2148007936 | bytes 10485760 | tf_op jit(solution)/shard_map/dot_general | solution.py:67
  322.8 2.6 copy.37
  325.5 2.4 multiply_convert_fusion.2
  328.8 1.9 fusion.11
  330.7 1.8 fusion.21
  334.0 2.3 copy.46
  336.3 114.1 %all-gather.7.cloned.1.call-done = f32[256,128,128]{2,1,0:T(8,128)} async-done(((f32[16,128,128]{2,1,0:T(8,128)}), f32[256,128,128]{2,1,0:T(8,128)}) %all-gather.7.cloned.1.call-update) | async-done | bytes 16777232 | tf_op jit(solution)/shard_map/all_gather | solution.py:34
  450.5 22.7 %while.23 = (s32[]{:T(128)}, f32[16,128,128]{2,1,0:T(8,128)S(1)}, s32[]{:T(128)}, f32[16,16,128,128]{3,2,1,0:T(8,128)}, s32[]{:T(128)}, /*index=5*/s32[]{:T(128)}, s32[]{:T(128)}, s32[]{:T(128)}) while((s32[]{:T(128)}, f32[16,128,128]{2,1,0:T(8,128)S(1)}, s32[]{:T(128)}, f32[16,16,128,128]{3,2,1,0:T(8,128)}, s32[]{:T(128)}, ...), condition=%wide.region_3.4_spmd, body=%wide.region_2.3_spmd.sunk | while | flops 262150 | bytes 3145871 | solution.py:41
  450.5 1.5 bitcast_add_fusion.8
  452.0 1.5 bitcast_add_fusion.8
  461.1 1.5 bitcast_add_fusion.8
  473.1 3.3 fusion.1
  476.5 2.3 copy.47
  478.7 3.1 add_convert_fusion
  481.8 2.3 copy.48
  484.1 1.8 convert_element_type.56
  (80 shorter events, 39.8 us)
Async XLA Ops:
  7.2 137.3 %copy-start = (bf16[1,256,2048]{2,1,0:T(8,128)(2,1)S(1)}, bf16[1,256,2048]{2,1,0:T(8,128)(2,1)}, u32[]{:S(2)}) copy-start(bf16[1,256,2048]{2,1,0:T(8,128)(2,1)} %param.12) | copy-start | bytes 3145732
  7.2 134.7 %all-gather.5.cloned.1.call-start = ((), (), s32[]{:S(2)}) async-start(), calls=%async_computation.4 | async-start | bytes 17825792 | tf_op jit(solution)/shard_map/all_gather | solution.py:34
  8.8 10.1 %copy-start.1 = (bf16[1,256,2048]{1,2,0:T(8,128)(2,1)}, bf16[1,256,2048]{1,2,0:T(8,128)(2,1)S(1)}, u32[]{:S(2)}) copy-start(bf16[1,256,2048]{1,2,0:T(8,128)(2,1)S(1)} %copy.53) | copy-start | bytes 3145732
  12.1 324.1 %reduce-scatter.3.cloned.1.call-start = ((), (), s32[]{:S(2)}) async-start(), calls=%async_computation.2 | async-start | bytes 8912896 | tf_op jit(solution)/shard_map/reduce_scatter | solution.py:89
  13.6 1.0 copy-start.2
  15.3 1.4 copy-start.5
  150.1 300.2 %all-gather.7.cloned.1.call-start = ((), (), s32[]{:S(2)}) async-start(), calls=%async_computation.5 | async-start | bytes 17825792 | tf_op jit(solution)/shard_map/all_gather | solution.py:34
  159.5 0.8 copy-start.9
  159.5 29.6 %collective-permute-start = (bf16[128,2048]{1,0:T(8,128)(2,1)S(1)}, bf16[128,2048]{1,0:T(8,128)(2,1)S(1)}, u32[]{:S(2)}, u32[]{:S(2)}) collective-permute-start(bf16[128,2048]{1,0:T(8,128)(2,1)S(1)} %all_gather.15), channel_id=1, source_target_pairs={{0,2},{2,4},{4,6},{6,8},{8,10},{10,12},{12,14},{14,16},{16,18},{18... | collective-permute-start | bytes 1572872 | tf_op jit(solution)/shard_map/ppermute | solution.py:20
  160.3 29.3 %collective-permute-start.1 = (bf16[128,2048]{1,0:T(8,128)(2,1)S(1)}, bf16[128,2048]{1,0:T(8,128)(2,1)S(1)}, u32[]{:S(2)}, u32[]{:S(2)}) collective-permute-start(bf16[128,2048]{1,0:T(8,128)(2,1)S(1)} %all_gather.15), channel_id=1, source_target_pairs={{0,30},{2,0},{4,2},{6,4},{8,6},{10,8},{12,10},{14,12},{16,14},{18,... | collective-permute-start | bytes 1572872 | tf_op jit(solution)/shard_map/ppermute | solution.py:23
  189.1 12.7 %copy-start.12 = (bf16[128,2048]{1,0:T(8,128)(2,1)}, bf16[128,2048]{1,0:T(8,128)(2,1)S(1)}, u32[]{:S(2)}) copy-start(bf16[128,2048]{1,0:T(8,128)(2,1)S(1)} %collective-permute-done) | copy-start | bytes 1572868
  189.1 11.5 %collective-permute-start.2 = (bf16[128,2048]{1,0:T(8,128)(2,1)S(1)}, bf16[128,2048]{1,0:T(8,128)(2,1)}, u32[]{:S(2)}, u32[]{:S(2)}) collective-permute-start(bf16[128,2048]{1,0:T(8,128)(2,1)S(1)} %collective-permute-done), channel_id=1, source_target_pairs={{0,2},{2,4},{4,6},{6,8},{8,10},{10,12},{12,14},{14,16},{16,18},{18... | collective-permute-start | bytes 1572872 | tf_op jit(solution)/shard_map/ppermute | solution.py:20
  189.6 0.8 copy-start.11
  190.4 11.4 %collective-permute-start.3 = (bf16[128,2048]{1,0:T(8,128)(2,1)S(1)}, bf16[128,2048]{1,0:T(8,128)(2,1)}, u32[]{:S(2)}, u32[]{:S(2)}) collective-permute-start(bf16[128,2048]{1,0:T(8,128)(2,1)S(1)} %collective-permute-done.1), channel_id=1, source_target_pairs={{0,30},{2,0},{4,2},{6,4},{8,6},{10,8},{12,10},{14,12},{16,14},{18,... | collective-permute-start | bytes 1572872 | tf_op jit(solution)/shard_map/ppermute | solution.py:23
  200.6 20.5 %collective-permute-start.4 = (bf16[128,2048]{1,0:T(8,128)(2,1)}, bf16[128,2048]{1,0:T(8,128)(2,1)}, u32[]{:S(2)}, u32[]{:S(2)}) collective-permute-start(bf16[128,2048]{1,0:T(8,128)(2,1)} %collective-permute-done.2), channel_id=1, source_target_pairs={{0,2},{2,4},{4,6},{6,8},{8,10},{10,12},{12,14},{14,16},{16,18},{18... | collective-permute-start | bytes 1572872 | tf_op jit(solution)/shard_map/ppermute | solution.py:20
  201.8 26.4 %collective-permute-start.5 = (bf16[128,2048]{1,0:T(8,128)(2,1)}, bf16[128,2048]{1,0:T(8,128)(2,1)}, u32[]{:S(2)}, u32[]{:S(2)}) collective-permute-start(bf16[128,2048]{1,0:T(8,128)(2,1)} %collective-permute-done.3), channel_id=1, source_target_pairs={{0,30},{2,0},{4,2},{6,4},{8,6},{10,8},{12,10},{14,12},{16,14},{18,... | collective-permute-start | bytes 1572872 | tf_op jit(solution)/shard_map/ppermute | solution.py:23
  206.6 18.8 %copy-start.10 = (bf16[128,2048]{1,0:T(8,128)(2,1)S(1)}, bf16[128,2048]{1,0:T(8,128)(2,1)}, u32[]{:S(2)}) copy-start(bf16[128,2048]{1,0:T(8,128)(2,1)} %copy-done.9) | copy-start | bytes 1572868
  221.1 23.4 %collective-permute-start.6 = (bf16[128,2048]{1,0:T(8,128)(2,1)}, bf16[128,2048]{1,0:T(8,128)(2,1)}, u32[]{:S(2)}, u32[]{:S(2)}) collective-permute-start(bf16[128,2048]{1,0:T(8,128)(2,1)} %collective-permute-done.4), channel_id=1, source_target_pairs={{0,2},{2,4},{4,6},{6,8},{8,10},{10,12},{12,14},{14,16},{16,18},{18... | collective-permute-start | bytes 1572872 | tf_op jit(solution)/shard_map/ppermute | solution.py:20
  228.2 20.1 %collective-permute-start.7 = (bf16[128,2048]{1,0:T(8,128)(2,1)}, bf16[128,2048]{1,0:T(8,128)(2,1)S(1)}, u32[]{:S(2)}, u32[]{:S(2)}) collective-permute-start(bf16[128,2048]{1,0:T(8,128)(2,1)} %collective-permute-done.5), channel_id=1, source_target_pairs={{0,30},{2,0},{4,2},{6,4},{8,6},{10,8},{12,10},{14,12},{16,14},{18,... | collective-permute-start | bytes 1572872 | tf_op jit(solution)/shard_map/ppermute | solution.py:23
  244.5 12.9 %collective-permute-start.8 = (bf16[128,2048]{1,0:T(8,128)(2,1)}, bf16[128,2048]{1,0:T(8,128)(2,1)S(1)}, u32[]{:S(2)}, u32[]{:S(2)}) collective-permute-start(bf16[128,2048]{1,0:T(8,128)(2,1)} %collective-permute-done.6), channel_id=1, source_target_pairs={{0,2},{2,4},{4,6},{6,8},{8,10},{10,12},{12,14},{14,16},{16,18},{18... | collective-permute-start | bytes 1572872 | tf_op jit(solution)/shard_map/ppermute | solution.py:20
  248.3 12.9 %collective-permute-start.9 = (bf16[128,2048]{1,0:T(8,128)(2,1)S(1)}, bf16[128,2048]{1,0:T(8,128)(2,1)S(1)}, u32[]{:S(2)}, u32[]{:S(2)}) collective-permute-start(bf16[128,2048]{1,0:T(8,128)(2,1)S(1)} %collective-permute-done.7), channel_id=1, source_target_pairs={{0,30},{2,0},{4,2},{6,4},{8,6},{10,8},{12,10},{14,12},{16,14},{18,... | collective-permute-start | bytes 1572872 | tf_op jit(solution)/shard_map/ppermute | solution.py:23
  257.4 21.7 %collective-permute-start.10 = (bf16[128,2048]{1,0:T(8,128)(2,1)S(1)}, bf16[128,2048]{1,0:T(8,128)(2,1)S(1)}, u32[]{:S(2)}, u32[]{:S(2)}) collective-permute-start(bf16[128,2048]{1,0:T(8,128)(2,1)S(1)} %collective-permute-done.8), channel_id=1, source_target_pairs={{0,2},{2,4},{4,6},{6,8},{8,10},{10,12},{12,14},{14,16},{16,18},{18... | collective-permute-start | bytes 1572872 | tf_op jit(solution)/shard_map/ppermute | solution.py:20
  261.2 21.4 %collective-permute-start.11 = (bf16[128,2048]{1,0:T(8,128)(2,1)S(1)}, bf16[128,2048]{1,0:T(8,128)(2,1)S(1)}, u32[]{:S(2)}, u32[]{:S(2)}) collective-permute-start(bf16[128,2048]{1,0:T(8,128)(2,1)S(1)} %collective-permute-done.9), channel_id=1, source_target_pairs={{0,30},{2,0},{4,2},{6,4},{8,6},{10,8},{12,10},{14,12},{16,14},{18,... | collective-permute-start | bytes 1572872 | tf_op jit(solution)/shard_map/ppermute | solution.py:23
  279.1 13.1 %collective-permute-start.12 = (bf16[128,2048]{1,0:T(8,128)(2,1)S(1)}, bf16[128,2048]{1,0:T(8,128)(2,1)S(1)}, u32[]{:S(2)}, u32[]{:S(2)}) collective-permute-start(bf16[128,2048]{1,0:T(8,128)(2,1)S(1)} %collective-permute-done.10), channel_id=1, source_target_pairs={{0,2},{2,4},{4,6},{6,8},{8,10},{10,12},{12,14},{14,16},{16,18},{18... | collective-permute-start | bytes 1572872 | tf_op jit(solution)/shard_map/ppermute | solution.py:20
  282.6 19.5 %collective-permute-start.13 = (bf16[128,2048]{1,0:T(8,128)(2,1)S(1)}, bf16[128,2048]{1,0:T(8,128)(2,1)S(1)}, u32[]{:S(2)}, u32[]{:S(2)}) collective-permute-start(bf16[128,2048]{1,0:T(8,128)(2,1)S(1)} %collective-permute-done.11), channel_id=1, source_target_pairs={{0,30},{2,0},{4,2},{6,4},{8,6},{10,8},{12,10},{14,12},{16,14},{18,... | collective-permute-start | bytes 1572872 | tf_op jit(solution)/shard_map/ppermute | solution.py:23
  292.2 21.5 %collective-permute-start.14 = (bf16[128,2048]{1,0:T(8,128)(2,1)S(1)}, bf16[128,2048]{1,0:T(8,128)(2,1)S(1)}, u32[]{:S(2)}, u32[]{:S(2)}) collective-permute-start(bf16[128,2048]{1,0:T(8,128)(2,1)S(1)} %collective-permute-done.12), channel_id=1, source_target_pairs={{0,2},{2,4},{4,6},{6,8},{8,10},{10,12},{12,14},{14,16},{16,18},{18... | collective-permute-start | bytes 1572872 | tf_op jit(solution)/shard_map/ppermute | solution.py:20
  314.5 6.8 %copy-start.3 = (bf16[32,8,16,128]{3,2,1,0:T(8,128)(2,1)S(1)}, bf16[32,8,16,128]{3,2,1,0:T(8,128)(2,1)}, u32[]{:S(2)}) copy-start(bf16[32,8,16,128]{3,2,1,0:T(8,128)(2,1)} %copy-done.2) | copy-start | bytes 3145732
  320.4 1.0 copy-start.7
  325.4 158.7 %reduce-scatter.5.cloned.1.call-start = ((), (), s32[]{:S(2)}) async-start(), calls=%async_computation.3 | async-start | bytes 786432 | tf_op jit(solution)/shard_map/reduce_scatter | solution.py:100
  325.5 3.3 copy-start.4
  325.5 5.2 %copy-start.6 = (bf16[16,256,256]{2,1,0:T(8,128)(2,1)S(1)}, bf16[16,256,256]{2,1,0:T(8,128)(2,1)}, u32[]{:S(2)}) copy-start(bf16[16,256,256]{2,1,0:T(8,128)(2,1)} %copy-done.5) | copy-start | bytes 6291460
  325.5 5.2 %copy-start.8 = (bf16[2048,256]{1,0:T(8,128)(2,1)S(1)}, bf16[2048,256]{1,0:T(8,128)(2,1)}, u32[]{:S(2)}) copy-start(bf16[2048,256]{1,0:T(8,128)(2,1)} %copy-done.7) | copy-start | bytes 3145732
Sparse Core Ops, SparseCore 0:
  12.2 129.5 all-gather.4
  150.2 158.7 reduce-scatter.2
  325.5 124.7 all-gather.6
  452.5 12.6 reduce-scatter.4
